TPU v7x, 32 devices: a whole 2x2x4 slice. The times are simulated.
32 devices in a mesh: dp: 2 (over core), row: 4 (over z), col: 4 (over y, x).
Axes of the slice: x: 2, y: 2, z: 4, core: 2. Of those that a mesh axis runs over, the one named last changes fastest.
Arguments:
- inputs: bfloat16 [512, 12288], P('dp', 'col'), may hold values from -6 to 6
- weight_tiles: bfloat16 [4, 4, 432, 4096], P('row', 'col', 'dp'), may hold values from -0.109375 to 0.109375
- tile_rows: int32 [4, 4, 432], P('row', 'col'), may hold values from 0 to 191, as said below
- tile_cols: int32 [4, 4, 432], P('row', 'col'), may hold values from 0 to 47, as said below
- tile_counts: int32 [4, 4], P('row', 'col'), may hold values from 54 to 432, as said below
- act_grad: bfloat16 [512, 49152], P('dp', ('row', 'col')), may hold values from -6 to 6
Outputs:
- activation: bfloat16 [512, 49152], P('dp', ('row', 'col'))
- input_grad: bfloat16 [512, 12288], P(('dp', 'row'), 'col')
- tile_grads: bfloat16 [4, 4, 432, 4096], P('row', 'col', 'dp')
Inputs may be any that keep to these rules, and one draw needn't show every extreme that they name: `tile_rows`: block row of a slot within its region; within each region the slots name distinct blocks. `tile_cols`: block column of a slot within its region. `tile_counts`: live slots of a region are its first ones; some region has all 432 slots live.
All inputs are finite; a program needn't handle non-finite values.
Results may differ from a plain program's by a relative error of at most 0.015.
Values may be sent and summed in bfloat16 or wider, within the bound.
No kernel may reach another device: no remote copies, remote signals or barrier semaphores. Data moves between devices by JAX's collectives and lax.ppermute only.
A program may use at most 128 MiB of HBM per device.

v0:
```python
import jax
import jax.numpy as jnp
from jax import lax
from jax.sharding import PartitionSpec as P

COEFF = 0.7978845608028654
CUBIC = 0.044715


def gelu_value(values):
    return 0.5 * values * (1.0 + jnp.tanh(COEFF * (values + CUBIC * values * values * values)))


def gelu_slope(values):
    inner = jnp.tanh(COEFF * (values + CUBIC * values * values * values))
    return 0.5 * (1.0 + inner) + 0.5 * values * (1.0 - inner * inner) * COEFF * (
        1.0 + 3.0 * CUBIC * values * values
    )


def group_loop(slot_count, advance, initial, widest):
    group_width = max((divisor for divisor in range(1, widest + 1) if slot_count % divisor == 0))

    def looped(group_index, running):
        return advance(running, group_index * group_width, group_width)

    return lax.fori_loop(0, slot_count // group_width, looped, initial)


def one_hot_rows(block_ids, block_total):
    return (block_ids[:, None] == jnp.arange(block_total)[None, :]).astype(jnp.bfloat16)


def pick_blocks(table, block_ids):
    selector = one_hot_rows(block_ids, table.shape[0])
    flat = table.reshape(table.shape[0], table.shape[1] * table.shape[2])
    picked = jnp.dot(selector, flat, preferred_element_type=jnp.float32).astype(jnp.bfloat16)
    return picked.reshape(block_ids.shape[0], table.shape[1], table.shape[2])


def place_blocks(running, products, block_ids):
    selector = one_hot_rows(block_ids, running.shape[0])
    flat = products.reshape(products.shape[0], products.shape[1] * products.shape[2])
    upper = flat.astype(jnp.bfloat16)
    lower = (flat - upper.astype(jnp.float32)).astype(jnp.bfloat16)
    added = jnp.dot(selector.T, upper, preferred_element_type=jnp.float32)
    added = added + jnp.dot(selector.T, lower, preferred_element_type=jnp.float32)
    return running + added.reshape(running.shape)


def local(inputs, weight_tiles, tile_rows, tile_cols, tile_counts, act_grad):
    token_count = inputs.shape[0]
    in_blocks = inputs.shape[1] // 64
    col_devices = lax.axis_size("col")
    share = act_grad.shape[1]
    out_blocks = share * col_devices // 64
    max_slots = tile_rows.shape[2]
    row_ids = tile_rows.reshape(max_slots)
    col_ids = tile_cols.reshape(max_slots)
    alive = (jnp.arange(max_slots) < tile_counts.reshape(())).astype(jnp.float32)
    input_blocks = inputs.T.reshape(in_blocks, 64, token_count)

    def slot_info(slot_start, group_width):
        rows_here = lax.dynamic_slice_in_dim(row_ids, slot_start, group_width)
        cols_here = lax.dynamic_slice_in_dim(col_ids, slot_start, group_width)
        alive_here = lax.dynamic_slice_in_dim(alive, slot_start, group_width)
        return (rows_here, cols_here, alive_here)

    empty_rows = jnp.zeros((out_blocks, 64, token_count), jnp.float32)
    piece = lax.all_gather(weight_tiles, "dp", axis=2, tiled=True)
    start = jnp.int32(0)
    piece_slots = piece.shape[2]
    piece_tiles = piece.reshape(piece_slots, 64, 64)

    def advance(inner_total, first, group_width):
        group_tiles = lax.dynamic_slice_in_dim(piece_tiles, first, group_width, 0)
        rows_here, cols_here, alive_here = slot_info(start + first, group_width)
        gathered = pick_blocks(input_blocks, cols_here)
        products = jnp.einsum(
            "sik,skt->sit", group_tiles, gathered, preferred_element_type=jnp.float32
        )
        products = products * alive_here[:, None, None]
        return place_blocks(inner_total, products, rows_here)

    pre_partial = group_loop(piece_slots, advance, empty_rows, 144)
    pre_partial = pre_partial.reshape(out_blocks * 64, token_count)
    pre_share = (
        lax.psum_scatter(pre_partial.astype(jnp.bfloat16), "col", scatter_dimension=0, tiled=True)
        .astype(jnp.float32)
        .T
    )
    activation = gelu_value(pre_share).astype(jnp.bfloat16)
    grad_share = (act_grad.astype(jnp.float32) * gelu_slope(pre_share)).astype(jnp.bfloat16)
    grad_full = lax.all_gather(grad_share, "col", axis=1, tiled=True)
    grad_blocks = grad_full.T.reshape(out_blocks, 64, token_count)
    empty_cols = jnp.zeros((in_blocks, 64, token_count), jnp.float32)
    piece = lax.all_gather(weight_tiles, "dp", axis=2, tiled=True)
    backward_start = jnp.int32(0)
    piece_slots = piece.shape[2]
    backward_piece_tiles = piece.reshape(piece_slots, 64, 64)

    def advance(inner_total, first, group_width):
        group_tiles = lax.dynamic_slice_in_dim(backward_piece_tiles, first, group_width, 0)
        rows_here, cols_here, alive_here = slot_info(backward_start + first, group_width)
        gathered = pick_blocks(grad_blocks, rows_here)
        products = jnp.einsum(
            "sik,sit->skt", group_tiles, gathered, preferred_element_type=jnp.float32
        )
        products = products * alive_here[:, None, None]
        return place_blocks(inner_total, products, cols_here)

    input_partial = group_loop(piece_slots, advance, empty_cols, 144)
    input_partial = input_partial.reshape(in_blocks * 64, token_count)
    input_grad = (
        lax.psum_scatter(input_partial.astype(jnp.bfloat16), "row", scatter_dimension=1, tiled=True)
        .astype(jnp.float32)
        .T.astype(jnp.bfloat16)
    )
    stored_slots = max_slots // lax.axis_size("dp")

    def advance(buffer, first, group_width):
        rows_here, cols_here, alive_here = slot_info(first, group_width)
        grads_here = pick_blocks(grad_blocks, rows_here)
        inputs_here = pick_blocks(input_blocks, cols_here)
        products = jnp.einsum(
            "sit,skt->sik", grads_here, inputs_here, preferred_element_type=jnp.float32
        )
        products = (products * alive_here[:, None, None]).reshape(group_width, 4096)
        return lax.dynamic_update_slice_in_dim(buffer, products, first, 0)

    tile_sum = lax.psum_scatter(
        group_loop(
            lax.axis_size("dp") * stored_slots,
            advance,
            jnp.zeros((lax.axis_size("dp") * stored_slots, 4096), jnp.float32),
            48,
        ).astype(jnp.bfloat16),
        "dp",
        scatter_dimension=0,
        tiled=True,
    )
    tile_grads = tile_sum.reshape(1, 1, stored_slots, 4096)
    return (activation, input_grad, tile_grads)


def solution(mesh):
    return jax.shard_map(
        local,
        mesh=mesh,
        in_specs=(
            P("dp", "col"),
            P("row", "col", "dp", None),
            P("row", "col", None),
            P("row", "col", None),
            P("row", "col"),
            P("dp", ("row", "col")),
        ),
        out_specs=(P("dp", ("row", "col")), P(("dp", "row"), "col"), P("row", "col", "dp", None)),
        check_vma=False,
    )
```

profile of v0, /device:TPU:0, one launch (start us, length us, event | category | flops | bytes accessed | tf_op | source)
XLA Modules:
  0.0 620.6 jit_solution(8441548578228094327)
XLA Ops:
  11.2 13.8 %all-gather.3.cloned.1.call-done = bf16[1,1,432,4096]{3,2,1,0:T(8,128)(2,1)} async-done(((bf16[1,1,216,4096]{3,2,1,0:T(8,128)(2,1)}), bf16[1,1,432,4096]{3,2,1,0:T(8,128)(2,1)}) %all-gather.3.cloned.1.call-update) | async-done | bytes 3538960 | tf_op jit(solution)/shard_map/all_gather | solution.py:70
  25.0 6.4 %copy.22 = bf16[1,1,432,4096]{2,3,1,0:T(8,128)(2,1)} copy(bf16[1,1,432,4096]{3,2,1,0:T(8,128)(2,1)} %all-gather.3.cloned.1.call-done) | data formatting | bytes 7077888 | tf_op jit(solution)/shard_map/all_gather | solution.py:70
  31.4 220.8 %while.45 = (s32[]{:T(128)}, f32[192,64,256]{2,1,0:T(8,128)}, s32[432]{0:T(512)S(1)}, bf16[432,64,64]{0,2,1:T(8,128)(2,1)}, s32[432]{0:T(512)S(1)}, /*index=5*/b...) while((s32[]{:T(128)}, f32[192,64,256]{2,1,0:T(8,128)}, ...), condition=%wide.wide.region_1.0_spmd.clone, body=%wide.wide.region_0.0_spmd.clone.sunk | while | flops 2366436096 | bytes 200939408 | solution.py:27
  33.0 3.5 copy.65
  39.0 3.8 copy.64
  42.9 3.7 broadcast_multiply_fusion.6
  46.6 11.4 %copy.66 = f32[18,8,64,256]{3,1,2,0:T(8,128)} copy(f32[18,8,64,256]{3,2,1,0:T(8,128)S(1)} %bitcast.144) | data formatting | bytes 18874368 | tf_op jit(solution)/shard_map/while
  58.0 5.6 fusion.72
  63.6 13.7 %convolution_add_fusion.6 = f32[192,16384]{1,0:T(8,128)} fusion(f32[192,16384]{1,0:T(8,128)S(1)} %fusion.72, f32[144,16384]{1,0:T(8,128)} %bitcast.142, s32[144]{0:T(256)S(1)} %dynamic_slice.115), kind=kOutput, calls=%fused_computation.8.clone.clone.1 | convolution fusion | flops 918580224 | bytes 34603584 | tf_op jit(solution)/shard_map/while/body/eval_jaxpr/dot_general | solution.py:47
  77.4 13.8 %copy.67 = f32[24,8,64,256]{3,2,1,0:T(8,128)} copy(f32[24,8,64,256]{3,1,2,0:T(8,128)} %bitcast.143) | data formatting | bytes 25165824 | tf_op jit(solution)/shard_map/while
  91.2 11.8 %bitcast_add_fusion.6 = f32[192,64,256]{2,1,0:T(8,128)} fusion(f32[24,8,64,256]{3,2,1,0:T(8,128)} %copy.67, f32[192,64,256]{2,1,0:T(8,128)} %get-tuple-element.774, pred[]{:T(512)S(6)} %compare.8), kind=kLoop, calls=%fused_computation.10.clone.clone.1 | loop fusion | flops 6291456 | bytes 37748736 | tf_op jit(solution)/shard_map/while/body/eval_jaxpr/add | solution.py:48
  104.5 3.5 copy.65
  108.1 2.5 constant_dynamic-slice_fusion.6
  110.5 3.8 copy.64
  114.4 3.7 broadcast_multiply_fusion.6
  118.1 11.4 %copy.66 = f32[18,8,64,256]{3,1,2,0:T(8,128)} copy(f32[18,8,64,256]{3,2,1,0:T(8,128)S(1)} %bitcast.144) | data formatting | bytes 18874368 | tf_op jit(solution)/shard_map/while
  129.6 5.6 fusion.72
  135.2 13.7 %convolution_add_fusion.6 = f32[192,16384]{1,0:T(8,128)} fusion(f32[192,16384]{1,0:T(8,128)S(1)} %fusion.72, f32[144,16384]{1,0:T(8,128)} %bitcast.142, s32[144]{0:T(256)S(1)} %dynamic_slice.115), kind=kOutput, calls=%fused_computation.8.clone.clone.1 | convolution fusion | flops 918580224 | bytes 34603584 | tf_op jit(solution)/shard_map/while/body/eval_jaxpr/dot_general | solution.py:47
  148.9 13.8 %copy.67 = f32[24,8,64,256]{3,2,1,0:T(8,128)} copy(f32[24,8,64,256]{3,1,2,0:T(8,128)} %bitcast.143) | data formatting | bytes 25165824 | tf_op jit(solution)/shard_map/while
  162.8 14.7 %bitcast_add_fusion.6 = f32[192,64,256]{2,1,0:T(8,128)} fusion(f32[24,8,64,256]{3,2,1,0:T(8,128)} %copy.67, f32[192,64,256]{2,1,0:T(8,128)} %get-tuple-element.774, pred[]{:T(512)S(6)} %compare.8), kind=kLoop, calls=%fused_computation.10.clone.clone.1 | loop fusion | flops 6291456 | bytes 37748736 | tf_op jit(solution)/shard_map/while/body/eval_jaxpr/add | solution.py:48
  179.0 3.5 copy.65
  185.0 3.8 copy.64
  188.8 3.7 broadcast_multiply_fusion.6
  192.6 11.4 %copy.66 = f32[18,8,64,256]{3,1,2,0:T(8,128)} copy(f32[18,8,64,256]{3,2,1,0:T(8,128)S(1)} %bitcast.144) | data formatting | bytes 18874368 | tf_op jit(solution)/shard_map/while
  204.0 5.6 fusion.72
  209.6 13.7 %convolution_add_fusion.6 = f32[192,16384]{1,0:T(8,128)} fusion(f32[192,16384]{1,0:T(8,128)S(1)} %fusion.72, f32[144,16384]{1,0:T(8,128)} %bitcast.142, s32[144]{0:T(256)S(1)} %dynamic_slice.115), kind=kOutput, calls=%fused_computation.8.clone.clone.1 | convolution fusion | flops 918580224 | bytes 34603584 | tf_op jit(solution)/shard_map/while/body/eval_jaxpr/dot_general | solution.py:47
  223.3 13.8 %copy.67 = f32[24,8,64,256]{3,2,1,0:T(8,128)} copy(f32[24,8,64,256]{3,1,2,0:T(8,128)} %bitcast.143) | data formatting | bytes 25165824 | tf_op jit(solution)/shard_map/while
  237.2 14.7 %bitcast_add_fusion.6 = f32[192,64,256]{2,1,0:T(8,128)} fusion(f32[24,8,64,256]{3,2,1,0:T(8,128)} %copy.67, f32[192,64,256]{2,1,0:T(8,128)} %get-tuple-element.774, pred[]{:T(512)S(6)} %compare.8), kind=kLoop, calls=%fused_computation.10.clone.clone.1 | loop fusion | flops 6291456 | bytes 37748736 | tf_op jit(solution)/shard_map/while/body/eval_jaxpr/add | solution.py:48
  252.2 8.2 %convert_element_type.122 = bf16[192,64,256]{2,1,0:T(8,128)(2,1)} convert(f32[192,64,256]{2,1,0:T(8,128)} %get-tuple-element.375) | non-fusion elementwise | flops 3145728 | bytes 18874368 | tf_op jit(solution)/shard_map/convert_element_type | solution.py:88
  262.6 69.4 %reduce-scatter.6.cloned.1.call-done = bf16[3072,256]{1,0:T(8,128)(2,1)} async-done(((bf16[12288,256]{1,0:T(8,128)(2,1)}), bf16[3072,256]{1,0:T(8,128)(2,1)}) %reduce-scatter.6.cloned.1.call-update) | async-done | bytes 1572880 | tf_op jit(solution)/shard_map/reduce_scatter | solution.py:88
  332.0 4.7 fusion.20
  338.9 68.1 %all-gather.5.cloned.1.call-done = bf16[256,12288]{0,1:T(8,128)(2,1)} async-done(((bf16[256,3072]{0,1:T(8,128)(2,1)}), bf16[256,12288]{0,1:T(8,128)(2,1)}) %all-gather.5.cloned.1.call-update) | async-done | bytes 6291472 | tf_op jit(solution)/shard_map/all_gather | solution.py:94
  407.0 10.5 %reshape_reshape.30 = bf16[192,16384]{1,0:T(8,128)(2,1)} reshape(bf16[12288,256]{1,0:T(8,128)(2,1)} %bitcast.156) | data formatting | bytes 12582912 | tf_op jit(solution)/shard_map/while/body/eval_jaxpr/reshape;reshape | solution.py:36
  417.5 10.4 %reshape_reshape.36 = bf16[192,16384]{1,0:T(8,128)(2,1)} reshape(bf16[12288,256]{1,0:T(8,128)(2,1)} %bitcast.157) | data formatting | bytes 12582912 | tf_op jit(solution)/shard_map/while/body/eval_jaxpr/reshape;reshape | solution.py:36
  427.9 98.9 %while.46 = (s32[]{:T(128)}, f32[48,64,256]{2,1,0:T(8,128)}, s32[432]{0:T(512)S(1)}, bf16[432,64,64]{0,2,1:T(8,128)(2,1)}, s32[432]{0:T(512)S(1)}, /*index=5*/bf...) while((s32[]{:T(128)}, f32[48,64,256]{2,1,0:T(8,128)}, ...), condition=%wide.wide.region_4.0_spmd.clone, body=%wide.wide.region_3.0_spmd.clone.sunk | while | flops 1679860224 | bytes 117577552 | solution.py:27
  428.2 4.2 convolution_convert_fusion.15
  432.4 3.6 copy.69
  437.1 4.5 copy.68
  441.7 4.4 broadcast_multiply_fusion.7
  446.1 7.7 %copy.70 = f32[18,8,64,256]{3,1,2,0:T(8,128)S(1)} copy(f32[18,8,64,256]{3,2,1,0:T(8,128)S(1)} %bitcast.145) | data formatting | bytes 18874368 | tf_op jit(solution)/shard_map/while
  457.2 2.5 bitcast_add_fusion.7
  459.8 4.2 convolution_convert_fusion.15
  464.0 3.6 copy.69
  468.7 4.5 copy.68
  473.3 4.4 broadcast_multiply_fusion.7
  477.8 7.7 %copy.70 = f32[18,8,64,256]{3,1,2,0:T(8,128)S(1)} copy(f32[18,8,64,256]{3,2,1,0:T(8,128)S(1)} %bitcast.145) | data formatting | bytes 18874368 | tf_op jit(solution)/shard_map/while
  488.8 4.4 bitcast_add_fusion.7
  493.3 4.2 convolution_convert_fusion.15
  497.5 3.6 copy.69
  502.2 4.5 copy.68
  506.8 4.4 broadcast_multiply_fusion.7
  511.2 7.7 %copy.70 = f32[18,8,64,256]{3,1,2,0:T(8,128)S(1)} copy(f32[18,8,64,256]{3,2,1,0:T(8,128)S(1)} %bitcast.145) | data formatting | bytes 18874368 | tf_op jit(solution)/shard_map/while
  522.2 4.4 bitcast_add_fusion.7
  533.0 69.1 %while.44 = (s32[]{:T(128)}, bf16[432,4096]{1,0:T(8,128)(2,1)}, s32[432]{0:T(512)S(1)}, bf16[12288,256]{1,0:T(8,128)(2,1)}, s32[432]{0:T(512)S(1)}, /*index=5*/b...) while((s32[]{:T(128)}, bf16[432,4096]{1,0:T(8,128)(2,1)}, ...), condition=%wide.wide.region_7.0_spmd, body=%wide.wide.region_6.0_spmd.sunk | while | flops 480128256 | bytes 22415228 | solution.py:27
  533.0 4.1 convolution_convert_fusion.12
  540.7 4.1 convolution_convert_fusion.12
  548.4 4.1 convolution_convert_fusion.12
  556.1 4.1 convolution_convert_fusion.12
  563.8 4.1 convolution_convert_fusion.12
  571.5 4.1 convolution_convert_fusion.12
  579.1 4.1 convolution_convert_fusion.12
  586.8 4.1 convolution_convert_fusion.12
  594.5 4.1 convolution_convert_fusion.12
  605.3 8.5 %reduce-scatter.8.cloned.1.call-done = bf16[216,4096]{1,0:T(8,128)(2,1)} async-done(((bf16[432,4096]{1,0:T(8,128)(2,1)}), bf16[216,4096]{1,0:T(8,128)(2,1)}) %reduce-scatter.8.cloned.1.call-update) | async-done | bytes 1769488 | tf_op jit(solution)/shard_map/reduce_scatter | solution.py:131
  (176 shorter events, 72.2 us)
Async XLA Ops:
  7.2 17.8 %all-gather.3.cloned.1.call-start = ((), (), s32[]{:S(2)}) async-start(), calls=%async_computation.3 | async-start | bytes 5308416 | tf_op jit(solution)/shard_map/all_gather | solution.py:70
  7.9 324.1 %reduce-scatter.6.cloned.1.call-start = ((), (), s32[]{:S(2)}) async-start(), calls=%async_computation.4 | async-start | bytes 7864320 | tf_op jit(solution)/shard_map/reduce_scatter | solution.py:88
  9.7 21.7 %copy-start.5 = (bf16[256,3072]{0,1:T(8,128)(2,1)}, bf16[256,3072]{0,1:T(8,128)(2,1)S(1)}, u32[]{:S(2)}) copy-start(bf16[256,3072]{0,1:T(8,128)(2,1)S(1)} %copy.23) | copy-start | bytes 4718596
  11.1 20.3 %copy-start.9 = (s32[1,1,432]{2,1,0:T(1,128)S(1)}, s32[1,1,432]{2,1,0:T(1,128)}, u32[]{:S(2)}) copy-start(s32[1,1,432]{2,1,0:T(1,128)} %param.14) | copy-start | bytes 5188
  11.1 20.3 %copy-start.10 = (s32[1,1,432]{2,1,0:T(1,128)S(1)}, s32[1,1,432]{2,1,0:T(1,128)}, u32[]{:S(2)}) copy-start(s32[1,1,432]{2,1,0:T(1,128)} %param.15) | copy-start | bytes 5188
  31.4 1.5 copy-start.3
  33.0 3.6 copy-start
  91.2 11.8 %copy-start.4 = (bf16[48,16384]{1,0:T(8,128)(2,1)S(1)}, bf16[48,16384]{1,0:T(8,128)(2,1)}, u32[]{:S(2)}) copy-start(bf16[48,16384]{1,0:T(8,128)(2,1)} %copy-done.3) | copy-start | bytes 4718596 | tf_op jit(solution)/shard_map/while
  103.0 1.5 copy-start.3
  104.5 3.6 copy-start
  162.8 14.7 %copy-start.4 = (bf16[48,16384]{1,0:T(8,128)(2,1)S(1)}, bf16[48,16384]{1,0:T(8,128)(2,1)}, u32[]{:S(2)}) copy-start(bf16[48,16384]{1,0:T(8,128)(2,1)} %copy-done.3) | copy-start | bytes 4718596 | tf_op jit(solution)/shard_map/while
  177.5 1.5 copy-start.3
  179.0 3.6 copy-start
  237.2 14.7 %copy-start.4 = (bf16[48,16384]{1,0:T(8,128)(2,1)S(1)}, bf16[48,16384]{1,0:T(8,128)(2,1)}, u32[]{:S(2)}) copy-start(bf16[48,16384]{1,0:T(8,128)(2,1)} %copy-done.3) | copy-start | bytes 4718596 | tf_op jit(solution)/shard_map/while
  260.5 1.4 copy-start.8
  260.5 146.5 %all-gather.5.cloned.1.call-start = ((), (), s32[]{:S(2)}) async-start(), calls=%async_computation.5 | async-start | bytes 7864320 | tf_op jit(solution)/shard_map/all_gather | solution.py:94
  262.6 74.2 %copy-start.6 = (bf16[3072,256]{1,0:T(8,128)(2,1)S(1)}, bf16[3072,256]{1,0:T(8,128)(2,1)}, u32[]{:S(2)}) copy-start(bf16[3072,256]{1,0:T(8,128)(2,1)} %get-tuple-element.884) | copy-start | bytes 4718596
  336.7 268.5 %reduce-scatter.10.cloned.1.call-start = ((), (), s32[]{:S(2)}) async-start(), calls=%async_computation.7 | async-start | bytes 1966080 | tf_op jit(solution)/shard_map/convert_element_type | solution.py:117
  432.4 3.6 copy-start.1
  464.0 3.6 copy-start.1
  497.5 3.6 copy-start.1
  530.7 2.3 copy-start.2
  530.7 83.0 %reduce-scatter.8.cloned.1.call-start = ((), (), s32[]{:S(2)}) async-start(), calls=%async_computation.6 | async-start | bytes 5308416 | tf_op jit(solution)/shard_map/reduce_scatter | solution.py:131
  602.1 1.4 copy-start.7
Sparse Core Ops, SparseCore 0:
  9.5 15.3 all-gather.2
  260.6 71.3 reduce-scatter.5
  336.8 70.1 all-gather.4
  530.9 35.3 reduce-scatter.9
  602.3 11.4 reduce-scatter.7
where the time goes:
time: 623 us; the launch traced here: 621 us
  local copies, waits for them, and re-layouts  223 us (36%)
  waiting for transfers between devices  161 us (26%)
  matrix products  153 us (25%)
  other arithmetic  67.6 us (11%)
  between operations  14.8 us (2%)
    while x60, local copies, waits for them, and re-layouts  130 us
    reduce_scatter x1, waiting for transfers between devices, local(): lax.psum_scatter(pre_partial.astype(jnp.bfloat16), 'col', scatter_dimensi...  69.4 us
    all_gather x1, waiting for transfers between devices, local(): grad_full = lax.all_gather(grad_share, 'col', axis=1, tiled=True)  68.1 us
    dot_general x24, matrix products, pick_blocks(): jnp.dot(selector, flat, preferred_element_type=jnp.float32)  59.2 us
    add x6, other arithmetic, place_blocks(): return running + added.reshape(running.shape)  52.6 us
    dot_general x6, matrix products, place_blocks(): jnp.dot(selector.T, lower, preferred_element_type=jnp.float32)  45.2 us
    another operation x4, local copies, waits for them, and re-layouts, pick_blocks(): flat = table.reshape(table.shape[0], table.shape[1] * table.shape[2])  23.8 us
    dot_general x6, matrix products, place_blocks(): added = jnp.dot(selector.T, upper, preferred_element_type=jnp.float32)  19.5 us
  transfers between devices with their start and end apart: 5, of which 4 were waited for; matrix products, arithmetic and copies ran while one was open for 13% of the time, Pallas kernels for 0%

commit v1 on v0

v1 whole, which is shorter than its diff:
```python
import functools

import jax
import jax.numpy as jnp
from jax import lax
from jax.experimental import pallas as pl
from jax.experimental.pallas import tpu as pltpu
from jax.sharding import PartitionSpec as P

COEFF = 0.7978845608028654
CUBIC = 0.044715
BLOCK = 64
VMEM_LIMIT = 60 * 1024 * 1024


def gelu_value(values):
    return 0.5 * values * (1.0 + jnp.tanh(COEFF * (values + CUBIC * values * values * values)))


def gelu_slope(values):
    inner = jnp.tanh(COEFF * (values + CUBIC * values * values * values))
    return 0.5 * (1.0 + inner) + 0.5 * values * (1.0 - inner * inner) * COEFF * (
        1.0 + 3.0 * CUBIC * values * values
    )


def widest_divisor(total, most):
    return max(divisor for divisor in range(1, most + 1) if total % divisor == 0)


def accumulate_kernel(unroll, count_ref, target_ref, source_ref, tiles_ref, table_ref, out_ref, total_ref):
    blocks = out_ref.shape[0]

    @pl.loop(0, blocks + 1)
    def _(block):
        total_ref[block] = jnp.zeros(total_ref.shape[1:], jnp.float32)

    count = count_ref[0]

    @pl.loop(0, pl.cdiv(count, unroll))
    def _(group):
        products = []
        places = []
        for lane in range(unroll):
            slot = group * unroll + lane
            places.append(jnp.where(slot < count, target_ref[slot], blocks))
            products.append(
                jnp.dot(tiles_ref[slot], table_ref[source_ref[slot]], preferred_element_type=jnp.float32)
            )
        for place, product in zip(places, products):
            total_ref[place] += product

    @pl.loop(0, blocks)
    def _(block):
        out_ref[block] = total_ref[block].astype(out_ref.dtype)


def accumulate(tiles, table, count, targets, sources, blocks):
    slots = tiles.shape[0]
    width = table.shape[2]
    whole = pl.BlockSpec(memory_space=pltpu.VMEM)
    scalars = pl.BlockSpec(memory_space=pltpu.SMEM)
    return pl.pallas_call(
        functools.partial(accumulate_kernel, widest_divisor(slots, 8)),
        out_shape=jax.ShapeDtypeStruct((blocks, BLOCK, width), jnp.bfloat16),
        in_specs=[scalars, scalars, scalars, whole, whole],
        out_specs=whole,
        scratch_shapes=[pltpu.VMEM((blocks + 1, BLOCK, width), jnp.float32)],
        compiler_params=pltpu.CompilerParams(vmem_limit_bytes=VMEM_LIMIT),
        cost_estimate=pl.CostEstimate(
            flops=2 * slots * BLOCK * BLOCK * width,
            bytes_accessed=2 * (tiles.size + table.size + blocks * BLOCK * width),
            transcendentals=0,
        ),
    )(count, targets, sources, tiles, table)


def outer_kernel(unroll, count_ref, row_ref, col_ref, grads_ref, inputs_ref, out_ref):
    slots = out_ref.shape[0]
    count = count_ref[0]

    @pl.loop(0, slots // unroll)
    def _(group):
        first = group * unroll

        @pl.when(first < count)
        def _():
            for lane in range(unroll):
                slot = first + lane
                product = jnp.dot(
                    grads_ref[row_ref[slot]], inputs_ref[col_ref[slot]], preferred_element_type=jnp.float32
                )
                out_ref[slot] = jnp.where(slot < count, product, 0.0).astype(out_ref.dtype)

        @pl.when(first >= count)
        def _():
            for lane in range(unroll):
                out_ref[first + lane] = jnp.zeros(out_ref.shape[1:], out_ref.dtype)


def outer(grads, inputs, count, rows, cols):
    slots = rows.shape[0]
    whole = pl.BlockSpec(memory_space=pltpu.VMEM)
    scalars = pl.BlockSpec(memory_space=pltpu.SMEM)
    return pl.pallas_call(
        functools.partial(outer_kernel, widest_divisor(slots, 8)),
        out_shape=jax.ShapeDtypeStruct((slots, BLOCK, BLOCK), jnp.bfloat16),
        in_specs=[scalars, scalars, scalars, whole, whole],
        out_specs=whole,
        compiler_params=pltpu.CompilerParams(vmem_limit_bytes=VMEM_LIMIT),
        cost_estimate=pl.CostEstimate(
            flops=2 * slots * BLOCK * BLOCK * grads.shape[2],
            bytes_accessed=2 * (grads.size + inputs.size + slots * BLOCK * BLOCK),
            transcendentals=0,
        ),
    )(count, rows, cols, grads, inputs)


def local(inputs, weight_tiles, tile_rows, tile_cols, tile_counts, act_grad):
    tokens = inputs.shape[0]
    in_blocks = inputs.shape[1] // BLOCK
    col_devices = lax.axis_size("col")
    share = act_grad.shape[1]
    out_blocks = share * col_devices // BLOCK
    slots = tile_rows.shape[2]
    rows = tile_rows.reshape(slots)
    cols = tile_cols.reshape(slots)
    count = tile_counts.reshape(1)

    inputs_t = inputs.T.reshape(in_blocks, BLOCK, tokens)
    tiles = lax.all_gather(weight_tiles, "dp", axis=2, tiled=True).reshape(slots, BLOCK, BLOCK)
    pre_partial = accumulate(tiles, inputs_t, count, rows, cols, out_blocks)
    pre = lax.psum_scatter(
        pre_partial.reshape(out_blocks * BLOCK, tokens), "col", scatter_dimension=0, tiled=True
    ).astype(jnp.float32)
    activation = gelu_value(pre).astype(jnp.bfloat16).T
    grad_share = (act_grad.T.astype(jnp.float32) * gelu_slope(pre)).astype(jnp.bfloat16)
    grads = lax.all_gather(grad_share, "col", axis=0, tiled=True).reshape(out_blocks, BLOCK, tokens)

    tiles_t = jnp.swapaxes(tiles, 1, 2)
    input_partial = accumulate(tiles_t, grads, count, cols, rows, in_blocks)
    input_grad = lax.psum_scatter(
        input_partial.reshape(in_blocks * BLOCK, tokens), "row", scatter_dimension=1, tiled=True
    ).T
    inputs_n = jnp.swapaxes(inputs_t, 1, 2)
    tile_partial = outer(grads, inputs_n, count, rows, cols).reshape(slots, BLOCK * BLOCK)
    tile_sum = lax.psum_scatter(tile_partial, "dp", scatter_dimension=0, tiled=True)
    tile_grads = tile_sum.reshape(1, 1, slots // lax.axis_size("dp"), BLOCK * BLOCK)
    return (activation, input_grad, tile_grads)


def solution(mesh):
    return jax.shard_map(
        local,
        mesh=mesh,
        in_specs=(
            P("dp", "col"),
            P("row", "col", "dp", None),
            P("row", "col", None),
            P("row", "col", None),
            P("row", "col"),
            P("dp", ("row", "col")),
        ),
        out_specs=(P("dp", ("row", "col")), P(("dp", "row"), "col"), P("row", "col", "dp", None)),
        check_vma=False,
    )
```

time: 623 us -> 300 us (0.48)
  local copies, waits for them, and re-layouts: 223 us -> 67 us
  matrix products: 153 us -> 0 us
  other arithmetic: 67.6 us -> 4.67 us
  Pallas kernels: 0 us -> 47 us
    dot_general x51 -> x0, matrix products: 153 us -> none  [the longest x24 59.2 us: pick_blocks(): jnp.dot(selector, flat, preferred_element_type=jnp.float32)]
    while x60 -> x0, local copies, waits for them, and re-layouts: 130 us -> none
    add x6 -> x0, other arithmetic: 52.6 us -> none  [place_blocks(): return running + added.reshape(running.shape)]
    pallas_call x0 -> x3, Pallas kernels: none -> 47 us  [the longest x2 31.3 us: accumulate(): pl.pallas_call(functools.partial(accumulate_kernel, widest_divisor(slots,...]
    dynamic_slice x57 -> x0, local copies, waits for them, and re-layouts: 38.9 us -> none  [the longest x6 18.7 us: advance(): group_tiles = lax.dynamic_slice_in_dim(piece_tiles, first, group_width, 0)]
    reshape x9 -> x5, local copies, waits for them, and re-layouts: 5.78 us -> 33.9 us  [the longest x2 19.7 us: local(): lax.all_gather(weight_tiles, 'dp', axis=2, tiled=True)]
    another operation x4 -> x0, local copies, waits for them, and re-layouts: 23.8 us -> none  [pick_blocks(): flat = table.reshape(table.shape[0], table.shape[1] * table.shape[2])]
    unnamed x5 -> x6, waiting for transfers between devices: 0.75 us -> 14.4 us
  transfers between devices with their start and end apart: 5 -> 5, of which waited for: 4 -> 5; matrix products, arithmetic and copies ran while one was open for 13% -> 11% of each run, Pallas kernels for 0% -> 5%
where the time goes in v1:
time: 300 us; the launch traced here: 298 us
  waiting for transfers between devices  165 us (55%)
  local copies, waits for them, and re-layouts  67 us (22%)
  Pallas kernels  47 us (16%)
  between operations  14.4 us (5%)
  other arithmetic  4.67 us (2%)
    reduce_scatter x1, waiting for transfers between devices, local(): lax.psum_scatter(pre_partial.reshape(out_blocks * BLOCK, tokens), 'col',...  73.7 us
    all_gather x1, waiting for transfers between devices, local(): lax.all_gather(grad_share, 'col', axis=0, tiled=True)  59.3 us
    pallas_call x2, Pallas kernels, accumulate(): pl.pallas_call(functools.partial(accumulate_kernel, widest_divisor(slots,...  31.3 us
    reshape x2, local copies, waits for them, and re-layouts, local(): lax.all_gather(weight_tiles, 'dp', axis=2, tiled=True)  19.7 us
    pallas_call x1, Pallas kernels, outer(): pl.pallas_call(functools.partial(outer_kernel, widest_divisor(slots, 8)),...  15.7 us
    unnamed x6, waiting for transfers between devices  14.4 us
    all_gather x1, waiting for transfers between devices, local(): lax.all_gather(weight_tiles, 'dp', axis=2, tiled=True)  13.8 us
    pallas_call x1, local copies, waits for them, and re-layouts, outer(): pl.pallas_call(functools.partial(outer_kernel, widest_divisor(slots, 8)),...  9.11 us
  transfers between devices with their start and end apart: 5, of which 5 were waited for; matrix products, arithmetic and copies ran while one was open for 11% of the time, Pallas kernels for 5%

profile of v1, /device:TPU:0, one launch (start us, length us, event | category | flops | bytes accessed | tf_op | source)
XLA Modules:
  0.0 298.1 jit_solution(13179151530763577627)
XLA Ops:
  7.2 0.0 all-gather.3.cloned.1.call-start
  7.2 0.7 all-gather.3.cloned.1.call-update
  7.9 0.0 reduce-scatter.6.cloned.1.call-start
  8.6 2.6 copy.25
  11.2 13.8 %all-gather.3.cloned.1.call-done = bf16[1,1,432,4096]{3,2,1,0:T(8,128)(2,1)} async-done(((bf16[1,1,216,4096]{3,2,1,0:T(8,128)(2,1)}), bf16[1,1,432,4096]{3,2,1,0:T(8,128)(2,1)}) %all-gather.3.cloned.1.call-update) | async-done | bytes 3538960 | tf_op jit(solution)/shard_map/all_gather | solution.py:131
  25.0 6.4 %copy.24 = bf16[1,1,432,4096]{2,3,1,0:T(8,128)(2,1)} copy(bf16[1,1,432,4096]{3,2,1,0:T(8,128)(2,1)} %all-gather.3.cloned.1.call-done) | data formatting | bytes 7077888 | tf_op jit(solution)/shard_map/all_gather | solution.py:131
  31.4 8.8 %copy.26.tiles_ref = bf16[432,64,64]{2,1,0:T(8,128)(2,1)} copy(bf16[432,64,64]{0,2,1:T(8,128)(2,1)} %bitcast.25) | data formatting | bytes 7077888 | tf_op jit(solution)/shard_map/reshape | solution.py:131
  40.2 16.7 %shard_map.85 = bf16[192,64,256]{2,1,0:T(8,128)(2,1)} custom-call(s32[1]{0:T(128)} %bitcast.20.count_ref, s32[432]{0:T(512)} %bitcast.34, s32[432]{0:T(512)} %bitcast.37, bf16[432,64,64]{2,1,0:T(8,128)(2,1)} %copy.26.tiles_ref, bf16[48,64,256]{2,1,0:T(8,128)(2,1)} %bitcast.30), custom_call_target="tpu_custom_call" | custom-call | flops 905969664 | bytes 11403264 | tf_op jit(solution)/shard_map/pallas_call | solution.py:63
  56.9 8.6 %copy.27 = bf16[12288,256]{0,1:T(8,128)(2,1)} copy(bf16[12288,256]{1,0:T(8,128)(2,1)} %bitcast.28) | data formatting | bytes 12582912 | tf_op jit(solution)/shard_map/reshape | solution.py:134
  65.5 0.0 copy-start.1
  65.5 0.0 reduce-scatter.6.cloned.1.call-update
  65.5 0.0 all-gather.5.cloned.1.call-start
  65.5 73.7 %reduce-scatter.6.cloned.1.call-done = bf16[3072,256]{0,1:T(8,128)(2,1)} async-done(((bf16[12288,256]{0,1:T(8,128)(2,1)}), bf16[3072,256]{0,1:T(8,128)(2,1)}) %reduce-scatter.6.cloned.1.call-update) | async-done | bytes 1572880 | tf_op jit(solution)/shard_map/reduce_scatter | solution.py:133
  139.2 0.0 copy-done.1
  139.2 4.7 %fusion.7 = (bf16[3072,256]{0,1:T(8,128)(2,1)}, bf16[256,3072]{1,0:T(8,128)(2,1)}) fusion(bf16[3072,256]{0,1:T(8,128)(2,1)} %reduce-scatter.6.cloned.1.call-done, bf16[256,3072]{1,0:T(8,128)(2,1)S(1)} %copy-done.1), kind=kLoop, calls=%fused_computation.14 | loop fusion | flops 18087936 | bytes 6291456 | tf_op jit(solution)/shard_map/convert_element_type | solution.py:137
  143.9 0.0 all-gather.5.cloned.1.call-update
  143.9 0.0 reduce-scatter.8.cloned.1.call-start
  144.0 10.9 %copy.28 = bf16[432,64,64]{1,2,0:T(8,128)(2,1)} copy(bf16[432,64,64]{0,2,1:T(8,128)(2,1)} %bitcast.26) | data formatting | bytes 7077888 | tf_op jit(solution)/shard_map/reshape | solution.py:131
  154.9 59.3 %all-gather.5.cloned.1.call-done = bf16[12288,256]{0,1:T(8,128)(2,1)} async-done(((bf16[3072,256]{0,1:T(8,128)(2,1)}), bf16[12288,256]{0,1:T(8,128)(2,1)}) %all-gather.5.cloned.1.call-update) | async-done | bytes 6291472 | tf_op jit(solution)/shard_map/all_gather | solution.py:138
  214.2 8.7 %copy.29 = bf16[12288,256]{1,0:T(8,128)(2,1)} copy(bf16[12288,256]{0,1:T(8,128)(2,1)} %all-gather.5.cloned.1.call-done) | data formatting | bytes 12582912 | tf_op jit(solution)/shard_map/all_gather | solution.py:138
  222.9 14.6 %shard_map.86 = bf16[48,64,256]{2,1,0:T(8,128)(2,1)} custom-call(s32[1]{0:T(128)} %bitcast.21.count_ref, s32[432]{0:T(512)} %bitcast.38, s32[432]{0:T(512)} %bitcast.35, bf16[432,64,64]{2,1,0:T(8,128)(2,1)} %bitcast.27, bf16[192,64,256]{2,1,0:T(8,128)(2,1)} %bitcast.23), custom_call_target="tpu_custom_call" | custom-call | flops 905969664 | bytes 11403264 | tf_op jit(solution)/shard_map/pallas_call | solution.py:63
  237.5 0.0 copy-start
  237.5 2.7 copy.30
  240.2 0.0 reduce-scatter.8.cloned.1.call-update
  240.3 0.0 reduce-scatter.10.cloned.1.call-start
  240.3 0.0 copy-done
  240.3 2.8 copy.31
  243.1 15.7 %shard_map.87 = bf16[432,64,64]{2,1,0:T(8,128)(2,1)} custom-call(s32[1]{0:T(128)} %bitcast.22.count_ref, s32[432]{0:T(512)} %bitcast.36, s32[432]{0:T(512)} %bitcast.39, bf16[192,64,256]{2,1,0:T(8,128)(2,1)} %bitcast.24, bf16[48,256,64]{2,1,0:T(8,128)(2,1)} %bitcast.32), custom_call_target="tpu_custom_call" | custom-call | flops 905969664 | bytes 11403264 | tf_op jit(solution)/shard_map/pallas_call | solution.py:105
  258.8 9.1 %copy.32 = bf16[432,64,64]{0,2,1:T(8,128)(2,1)} copy(bf16[432,64,64]{2,1,0:T(8,128)(2,1)} %shard_map.87) | data formatting | bytes 7077888 | tf_op jit(solution)/shard_map/pallas_call | solution.py:105
  267.9 6.4 %copy.34 = bf16[432,4096]{1,0:T(8,128)(2,1)} copy(bf16[432,4096]{0,1:T(8,128)(2,1)} %bitcast.29) | data formatting | bytes 7077888
  274.3 0.0 reduce-scatter.10.cloned.1.call-update
  274.4 3.5 %reduce-scatter.8.cloned.1.call-done = bf16[3072,64]{0,1:T(8,128)(2,1)} async-done(((bf16[3072,256]{0,1:T(8,128)(2,1)}), bf16[3072,64]{0,1:T(8,128)(2,1)}) %reduce-scatter.8.cloned.1.call-update) | async-done | bytes 393232 | tf_op jit(solution)/shard_map/reduce_scatter | solution.py:142
  277.9 13.7 %reduce-scatter.10.cloned.1.call-done = bf16[216,4096]{1,0:T(8,128)(2,1)} async-done(((bf16[432,4096]{1,0:T(8,128)(2,1)}), bf16[216,4096]{1,0:T(8,128)(2,1)}) %reduce-scatter.10.cloned.1.call-update) | async-done | bytes 1769488
Async XLA Ops:
  7.2 17.8 %all-gather.3.cloned.1.call-start = ((), (), s32[]{:S(2)}) async-start(), calls=%async_computation.3 | async-start | bytes 5308416 | tf_op jit(solution)/shard_map/all_gather | solution.py:131
  7.9 131.3 %reduce-scatter.6.cloned.1.call-start = ((), (), s32[]{:S(2)}) async-start(), calls=%async_computation.4 | async-start | bytes 7864320 | tf_op jit(solution)/shard_map/reduce_scatter | solution.py:133
  65.5 73.8 %copy-start.1 = (bf16[256,3072]{1,0:T(8,128)(2,1)S(1)}, bf16[256,3072]{1,0:T(8,128)(2,1)}, u32[]{:S(2)}) copy-start(bf16[256,3072]{1,0:T(8,128)(2,1)} %param.11) | copy-start | bytes 4718596
  65.5 148.8 %all-gather.5.cloned.1.call-start = ((), (), s32[]{:S(2)}) async-start(), calls=%async_computation.5 | async-start | bytes 7864320 | tf_op jit(solution)/shard_map/all_gather | solution.py:138
  143.9 134.0 %reduce-scatter.8.cloned.1.call-start = ((), (), s32[]{:S(2)}) async-start(), calls=%async_computation.6 | async-start | bytes 1966080 | tf_op jit(solution)/shard_map/reduce_scatter | solution.py:142
  237.5 2.8 copy-start
  240.3 51.4 %reduce-scatter.10.cloned.1.call-start = ((), (), s32[]{:S(2)}) async-start(), calls=%async_computation.7 | async-start | bytes 5308416
Sparse Core Ops, SparseCore 0:
  9.5 15.3 all-gather.2
  65.6 73.5 reduce-scatter.5
  144.1 70.1 all-gather.4
  240.4 37.4 reduce-scatter.7
  280.6 10.9 reduce-scatter.9
